TPU v7x, 128 devices: a whole 4x4x4 slice. The times are simulated.
128 devices in a mesh: req: 16 (over y, x), seq: 8 (over z, core).
Axes of the slice: x: 4, y: 4, z: 4, core: 2. Of those that a mesh axis runs over, the one named last changes fastest.
Arguments:
- qkv_proj: bfloat16 [16, 1024, 4096], P('req', 'seq'), may hold values from -6 to 6
- gate_proj: bfloat16 [16, 1024, 2048], P('req', 'seq'), may hold values from -6 to 6
- residual: bfloat16 [16, 1024, 2048], P('req', 'seq'), may hold values from -6 to 6
- log_decay: float32 [16, 1024, 8], P('req', 'seq'), may hold values from -1 to 0, as said below
- beta_logit: bfloat16 [16, 1024, 8], P('req', 'seq'), may hold values from -6 to 6
- lengths: int32 [16], replicated, may hold values from 1 to 1024, 8192 in all
- slot_request: int32 [16], replicated, may hold values from 0 to 15, each once
- conv_weight: float32 [4, 4096], replicated, may hold values from -3 to 3
- norm_gain: float32 [256], replicated, may hold values from 0.1 to 1.9
- out_weight: bfloat16 [2048, 2048], P(('req', 'seq')), may hold values from -0.125 to 0.125
- mlp_gain: float32 [2048], replicated, may hold values from 0.1 to 1.9
- w_gate: bfloat16 [2048, 5632], P('req', 'seq'), may hold values from -0.125 to 0.125
- w_up: bfloat16 [2048, 5632], P('req', 'seq'), may hold values from -0.125 to 0.125
- w_down: bfloat16 [5632, 2048], P('seq', 'req'), may hold values from -0.078125 to 0.078125
Outputs:
- hidden_out: bfloat16 [16, 1024, 2048], P('req', 'seq')
- final_state: float32 [16, 8, 128, 256], P('req', 'seq')
- conv_edge: bfloat16 [16, 3, 4096], P('req', None, 'seq')
Inputs may be any that keep to these rules, and one draw needn't show every extreme that they name: Slot s of the req axis holds request slot_request[s]. The 16 lengths sum to 8192, and the longest is exactly 1024. `log_decay`: every entry is negative.
All inputs are finite; a program needn't handle non-finite values.
Results may differ from a plain program's by a relative error of at most 0.014.
Values may be sent and summed in bfloat16 or wider, within the bound.
A program may use at most 128 MiB of HBM per device.

v0:
```python
import jax
import jax.numpy as jnp
from jax import lax
from jax.sharding import PartitionSpec as P

LOCAL_HEADS = 8
DK = 128
DV = 256
CONV = 4
BLOCK = 64
HK = 1024
EPS_NORM = 1e-05
EPS_UNIT = 1e-06
HIGHEST = lax.Precision.HIGHEST


def shifted(value, axis, steps):
    count = lax.axis_size(axis)
    initial, last = (max(0, -steps), min(count, count - steps))
    return lax.ppermute(value, axis, [(source, source + steps) for source in range(initial, last)])


def unit_norm(vector):
    return vector * lax.rsqrt(jnp.sum(vector * vector, axis=-1, keepdims=True) + EPS_UNIT)


def to_blocks(tensor, block_len):
    length = tensor.shape[0]
    grouped = tensor.reshape((length // block_len, block_len) + tensor.shape[1:])
    return jnp.moveaxis(grouped, 2, 0)


def block_tables(query_vec, key_vecs, beta_gate, decay_log, block_len):
    query_b = to_blocks(query_vec, block_len)
    keys_b = to_blocks(key_vecs, block_len)
    beta_b = to_blocks(beta_gate, block_len)
    cumulative = jnp.cumsum(to_blocks(decay_log, block_len), axis=-1)
    spread = cumulative[..., :, None] - cumulative[..., None, :]
    lower_full = jnp.tril(jnp.ones((block_len, block_len), jnp.float32))
    lower_strict = jnp.tril(jnp.ones((block_len, block_len), jnp.float32), -1)
    within = jnp.exp(jnp.where(lower_full > 0, spread, 0.0)) * lower_full
    key_inner = jnp.einsum("hnik,hnjk->hnij", keys_b, keys_b, precision=HIGHEST)
    couple = beta_b[..., :, None] * within * lower_strict * key_inner
    identity = jnp.broadcast_to(jnp.eye(block_len, dtype=jnp.float32), couple.shape)
    inverse = lax.linalg.triangular_solve(
        identity + couple, identity, left_side=True, lower=True, unit_diagonal=True
    )
    growth = jnp.exp(cumulative)
    weighted_keys = jnp.einsum(
        "hnij,hnjk->hnik", inverse, (beta_b * growth)[..., None] * keys_b, precision=HIGHEST
    )
    query_keys = jnp.einsum("hnik,hnjk->hnij", query_b, keys_b, precision=HIGHEST) * within
    grown_query = growth[..., None] * query_b
    keys_to_end = jnp.exp(cumulative[..., -1:] - cumulative)[..., None] * keys_b
    end_growth = growth[..., -1]
    return (inverse, beta_b, (weighted_keys, query_keys, grown_query, keys_to_end, end_growth))


def solve_values(inverse, beta_b, values_b):
    return jnp.einsum("hnij,hnjx->hnix", inverse, beta_b[..., None] * values_b, precision=HIGHEST)


def run_blocks(initial, solved, tables):
    weighted_keys, query_keys, grown_query, keys_to_end, end_growth = tables
    sequence = tuple(
        (
            jnp.moveaxis(tensor, 1, 0)
            for tensor in (solved, weighted_keys, query_keys, grown_query, keys_to_end, end_growth)
        )
    )

    def advance(running, inputs_now):
        solved_now, weighted_now, inner_now, query_now, keys_now, growth_now = inputs_now
        corrected = solved_now - jnp.einsum(
            "hck,hkx->hcx", weighted_now, running, precision=HIGHEST
        )
        output_now = jnp.einsum("hck,hkx->hcx", query_now, running, precision=HIGHEST) + jnp.einsum(
            "hcd,hdx->hcx", inner_now, corrected, precision=HIGHEST
        )
        running = growth_now[:, None, None] * running + jnp.einsum(
            "hck,hcx->hkx", keys_now, corrected, precision=HIGHEST
        )
        return (running, output_now)

    return lax.scan(advance, initial, sequence)


def local(
    qkv_proj,
    gate_proj,
    residual,
    log_decay,
    beta_logit,
    lengths,
    slot_request,
    conv_weight,
    norm_gain,
    out_weight,
    mlp_gain,
    w_gate,
    w_up,
    w_down,
):
    seq_index = lax.axis_index("seq")
    req_index = lax.axis_index("req")
    seq_size = lax.axis_size("seq")
    piece_len = qkv_proj.shape[1]
    channels = qkv_proj.shape[2]
    request_ids = jnp.arange(slot_request.shape[0], dtype=jnp.int32)
    request = jnp.sum(jnp.where(request_ids == req_index, slot_request, 0))
    length = jnp.sum(jnp.where(request_ids == request, lengths, 0))
    position = seq_index * piece_len + jnp.arange(piece_len, dtype=jnp.int32)
    live_mask = position < length
    tokens = qkv_proj[0]
    rim_rows = shifted(tokens[piece_len - (CONV - 1) :], "seq", 1)
    extended = jnp.concatenate([rim_rows, tokens], axis=0)
    convolved = jnp.zeros((piece_len, channels), jnp.float32)
    for offset in range(CONV):
        convolved = convolved + conv_weight[offset] * extended[offset : offset + piece_len].astype(
            jnp.float32
        )
    activated = jax.nn.silu(convolved)
    query_vec = unit_norm(activated[:, :HK].reshape(piece_len, LOCAL_HEADS, DK)) * DK ** (-0.5)
    key_vecs = unit_norm(activated[:, HK : 2 * HK].reshape(piece_len, LOCAL_HEADS, DK))
    values = activated[:, 2 * HK :].reshape(piece_len, LOCAL_HEADS, DV)
    beta_gate = jax.nn.sigmoid(beta_logit[0].astype(jnp.float32)) * live_mask[:, None]
    decay_log = jnp.where(live_mask[:, None], log_decay[0], 0.0)
    inverse, beta_b, tables = block_tables(query_vec, key_vecs, beta_gate, decay_log, BLOCK)
    values_b = to_blocks(values, BLOCK)
    solved = solve_values(inverse, beta_b, values_b)
    zero_state = jnp.zeros((LOCAL_HEADS, DK, DV), jnp.float32)
    incoming = zero_state
    for section_index in range(seq_size - 1):
        ending, discarded = run_blocks(incoming, solved, tables)
        incoming = shifted(ending.astype(jnp.bfloat16), "seq", 1).astype(ending.dtype)
    ending, outputs = run_blocks(incoming, solved, tables)
    outputs = jnp.moveaxis(outputs, 1, 2).reshape(piece_len, LOCAL_HEADS, DV)
    is_last = seq_index == seq_size - 1
    state_term = jnp.where(is_last, ending, 0.0)
    targets = length - (CONV - 1) + jnp.arange(CONV - 1, dtype=jnp.int32)
    select = (position[None, :] == targets[:, None]).astype(jnp.bfloat16)
    edge_term = jnp.dot(select, tokens, preferred_element_type=jnp.float32)
    state_part, edge_part = (
        lax.psum_scatter(
            state_term.astype(jnp.bfloat16), "seq", scatter_dimension=0, tiled=True
        ).astype(jnp.float32),
        lax.psum_scatter(
            edge_term.astype(jnp.bfloat16), "seq", scatter_dimension=1, tiled=True
        ).astype(jnp.float32),
    )
    gate_values = gate_proj[0].astype(jnp.float32).reshape(piece_len, LOCAL_HEADS, DV)
    scaled = outputs * lax.rsqrt(jnp.mean(outputs * outputs, axis=-1, keepdims=True) + EPS_NORM)
    mixed_heads = (
        (scaled * norm_gain * jax.nn.silu(gate_values))
        .reshape(piece_len, LOCAL_HEADS * DV)
        .astype(jnp.bfloat16)
    )
    attended = jnp.dot(
        mixed_heads,
        lax.all_gather(out_weight, ("req", "seq"), axis=0, tiled=True),
        preferred_element_type=jnp.float32,
    )
    hidden_state = (residual[0].astype(jnp.float32) + attended).astype(jnp.bfloat16)
    stream = hidden_state.astype(jnp.float32)
    normed = (
        stream * lax.rsqrt(jnp.mean(stream * stream, axis=-1, keepdims=True) + EPS_NORM) * mlp_gain
    ).astype(jnp.bfloat16)
    gate_full, up_full = (
        lax.all_gather(w_gate, "req", axis=0, tiled=True),
        lax.all_gather(w_up, "req", axis=0, tiled=True),
    )
    down_full = lax.all_gather(w_down, "req", axis=1, tiled=True)
    shard_rows = lax.all_gather(normed, "seq", axis=0, tiled=True)
    gate_part = jnp.dot(shard_rows, gate_full, preferred_element_type=jnp.float32)
    upward = jnp.dot(shard_rows, up_full, preferred_element_type=jnp.float32)
    inner_units = (jax.nn.silu(gate_part) * upward).astype(jnp.bfloat16)
    summed = lax.psum_scatter(
        jnp.dot(inner_units, down_full, preferred_element_type=jnp.float32).astype(jnp.bfloat16),
        "seq",
        scatter_dimension=0,
        tiled=True,
    ).astype(jnp.float32)
    combined = stream + summed
    hidden_out = jnp.where(live_mask[:, None], combined, 0.0).astype(jnp.bfloat16)
    return (hidden_out[None], state_part[None], edge_part.astype(jnp.bfloat16)[None])


def solution(mesh):
    return jax.shard_map(
        local,
        mesh=mesh,
        in_specs=(
            P("req", "seq", None),
            P("req", "seq", None),
            P("req", "seq", None),
            P("req", "seq", None),
            P("req", "seq", None),
            P(),
            P(),
            P(),
            P(),
            P(("req", "seq"), None),
            P(),
            P("req", "seq"),
            P("req", "seq"),
            P("seq", "req"),
        ),
        out_specs=(P("req", "seq", None), P("req", "seq", None, None), P("req", None, "seq")),
        check_vma=False,
    )
```

profile of v0, /device:TPU:0, one launch (start us, length us, event | category | flops | bytes accessed | tf_op | source)
XLA Modules:
  0.0 511.9 jit_solution(8159952312244182873)
XLA Ops:
  12.3 1.9 fusion.106
  17.2 3.4 divide_multiply_fusion
  20.6 1.4 multiply_bitcast_fusion
  23.9 1.8 fusion.72
  25.7 80.0 %custom-call.3 = f32[8,2,1,64,64]{3,4,2,1,0:T(8,128)} custom-call(f32[8,2,1,64,64]{4,3,2,1,0:T(8,128)} %fusion.72), custom_call_target="InvertDiagBlocksLowerTriangular" | custom-call | tf_op jit(solution)/shard_map/triangular_solve | solution.py:45
  105.7 2.0 fusion.85
  107.8 1.7 convolution_bitcast_fusion.2
  111.8 4.1 while.90
  116.8 5.9 %collective-permute-start.1 = (bf16[8,128,256]{2,1,0:T(8,128)(2,1)}, bf16[8,128,256]{2,1,0:T(8,128)(2,1)}, u32[]{:S(2)}, u32[]{:S(2)}) collective-permute-start(bf16[8,128,256]{2,1,0:T(8,128)(2,1)} %convert_element_type.129), channel_id=1, source_target_pairs={{0,1},{1,2},{2,3},{3,4},{4,5},{5,6},{6,7},{8,9},{9,10},{10,11},{11... | collective-permute-start | bytes 1572872 | tf_op jit(solution)/shard_map/ppermute | solution.py:20
  124.5 4.2 while.83
  125.3 1.3 convolution_add_fusion.18
  127.4 1.3 convolution_add_fusion.18
  129.6 7.3 %collective-permute-start.2 = (bf16[8,128,256]{2,1,0:T(8,128)(2,1)}, bf16[8,128,256]{2,1,0:T(8,128)(2,1)}, u32[]{:S(2)}, u32[]{:S(2)}) collective-permute-start(bf16[8,128,256]{2,1,0:T(8,128)(2,1)} %convert_element_type.131), channel_id=1, source_target_pairs={{0,1},{1,2},{2,3},{3,4},{4,5},{5,6},{6,7},{8,9},{9,10},{10,11},{11... | collective-permute-start | bytes 1572872 | tf_op jit(solution)/shard_map/ppermute | solution.py:20
  139.1 4.2 while.84
  139.8 1.3 convolution_add_fusion.19
  144.2 9.7 %collective-permute-start.3 = (bf16[8,128,256]{2,1,0:T(8,128)(2,1)}, bf16[8,128,256]{2,1,0:T(8,128)(2,1)}, u32[]{:S(2)}, u32[]{:S(2)}) collective-permute-start(bf16[8,128,256]{2,1,0:T(8,128)(2,1)} %convert_element_type.133), channel_id=1, source_target_pairs={{0,1},{1,2},{2,3},{3,4},{4,5},{5,6},{6,7},{8,9},{9,10},{10,11},{11... | collective-permute-start | bytes 1572872 | tf_op jit(solution)/shard_map/ppermute | solution.py:20
  156.1 4.2 while.85
  161.2 9.7 %collective-permute-start.4 = (bf16[8,128,256]{2,1,0:T(8,128)(2,1)}, bf16[8,128,256]{2,1,0:T(8,128)(2,1)}, u32[]{:S(2)}, u32[]{:S(2)}) collective-permute-start(bf16[8,128,256]{2,1,0:T(8,128)(2,1)} %convert_element_type.135), channel_id=1, source_target_pairs={{0,1},{1,2},{2,3},{3,4},{4,5},{5,6},{6,7},{8,9},{9,10},{10,11},{11... | collective-permute-start | bytes 1572872 | tf_op jit(solution)/shard_map/ppermute | solution.py:20
  173.2 4.2 while.86
  178.3 9.7 %collective-permute-start.5 = (bf16[8,128,256]{2,1,0:T(8,128)(2,1)}, bf16[8,128,256]{2,1,0:T(8,128)(2,1)}, u32[]{:S(2)}, u32[]{:S(2)}) collective-permute-start(bf16[8,128,256]{2,1,0:T(8,128)(2,1)} %convert_element_type.137), channel_id=1, source_target_pairs={{0,1},{1,2},{2,3},{3,4},{4,5},{5,6},{6,7},{8,9},{9,10},{10,11},{11... | collective-permute-start | bytes 1572872 | tf_op jit(solution)/shard_map/ppermute | solution.py:20
  190.2 4.2 while.87
  195.2 9.7 %collective-permute-start.6 = (bf16[8,128,256]{2,1,0:T(8,128)(2,1)}, bf16[8,128,256]{2,1,0:T(8,128)(2,1)}, u32[]{:S(2)}, u32[]{:S(2)}) collective-permute-start(bf16[8,128,256]{2,1,0:T(8,128)(2,1)} %convert_element_type.139), channel_id=1, source_target_pairs={{0,1},{1,2},{2,3},{3,4},{4,5},{5,6},{6,7},{8,9},{9,10},{10,11},{11... | collective-permute-start | bytes 1572872 | tf_op jit(solution)/shard_map/ppermute | solution.py:20
  206.9 1.9 copy.258
  210.0 4.2 while.88
  210.7 1.3 convolution_add_fusion.23
  212.8 1.3 convolution_add_fusion.23
  214.2 6.3 %collective-permute-start.7 = (bf16[8,128,256]{2,1,0:T(8,128)(2,1)S(1)}, bf16[8,128,256]{2,1,0:T(8,128)(2,1)S(1)}, u32[]{:S(2)}, u32[]{:S(2)}) collective-permute-start(bf16[8,128,256]{2,1,0:T(8,128)(2,1)S(1)} %convert_element_type.141), channel_id=1, source_target_pairs={{0,1},{1,2},{2,3},{3,4},{4,5},{5,6},{6,7},{8,9},{9,10},{10,11},{11... | collective-permute-start | bytes 1572872 | tf_op jit(solution)/shard_map/ppermute | solution.py:20
  222.9 1.9 fusion.70
  224.9 10.8 %while.89 = (s32[]{:T(128)}, f32[8,128,256]{2,1,0:T(8,128)S(1)}, f32[2,8,64,256]{3,2,1,0:T(8,128)}, f32[2,8]{1,0:T(2,128)S(1)}, f32[2,8,64,128]{3,2,1,0:T(8,128)...) while((s32[]{:T(128)}, f32[8,128,256]{2,1,0:T(8,128)S(1)}, ...), condition=%wide.region_20.21_spmd, body=%wide.region_19.20_spmd.sunk | while | flops 705429504 | bytes 19925256 | solution.py:85
  225.7 1.5 fusion.223
  231.1 1.5 fusion.223
  235.8 1.5 multiply_reduce_fusion.1
  237.6 1.4 copy.261
  239.6 1.3 copy.260
  241.0 5.8 %multiply_reduce_fusion = (f32[128]{0:T(128)S(1)}, f32[128,2048]{1,0:T(8,128)S(1)}) fusion(bf16[2048,2048]{1,0:T(8,128)(2,1)} %all-gather.6.cloned.1.call-done, f32[128,2048]{1,0:T(8,128)} %bitcast.348, f32[128,2048]{1,0:T(8,128)} %bitcast.347, bf16[1,128,2048]{2,1,0:T(8,128)(2,1)} %param.31, f32[2048]{0:T(1024)S(1)} %bitcast.360, ...), kind=kOutput, calls=%fused_computation.125 | convolution fusion | flops 1077673856 | bytes 12591616 | tf_op jit(solution)/shard_map/dot_general | solution.py:158
  249.9 1.4 copy.250
  252.6 6.2 %all-gather.10.cloned.1.call-done = bf16[2048,704]{0,1:T(8,128)(2,1)} async-done(((bf16[128,704]{0,1:T(8,128)(2,1)}), bf16[2048,704]{0,1:T(8,128)(2,1)}) %all-gather.10.cloned.1.call-update) | async-done | bytes 2883600 | tf_op jit(solution)/shard_map/all_gather | solution.py:169
  258.8 34.0 %all-gather.8.cloned.1.call-done = bf16[1024,2048]{1,0:T(8,128)(2,1)} async-done(((bf16[128,2048]{1,0:T(8,128)(2,1)}), bf16[1024,2048]{1,0:T(8,128)(2,1)}) %all-gather.8.cloned.1.call-update) | async-done | bytes 4194320 | tf_op jit(solution)/shard_map/all_gather | solution.py:173
  292.8 7.8 %fusion.114 = f32[1024,704]{0,1:T(8,128)} fusion(bf16[1024,2048]{1,0:T(8,128)(2,1)} %all-gather.8.cloned.1.call-done, bf16[2048,704]{0,1:T(8,128)(2,1)} %all-gather.10.cloned.1.call-done), kind=kOutput, calls=%fused_computation.195 | convolution fusion | flops 2952790016 | bytes 9961472 | tf_op jit(solution)/shard_map/dot_general | solution.py:174
  300.7 44.4 %all-gather.12.cloned.1.call-done = bf16[2048,704]{0,1:T(8,128)(2,1)} async-done(((bf16[128,704]{0,1:T(8,128)(2,1)}), bf16[2048,704]{0,1:T(8,128)(2,1)}) %all-gather.12.cloned.1.call-update) | async-done | bytes 2883600 | tf_op jit(solution)/shard_map/all_gather | solution.py:170
  345.1 51.8 %all-gather.14.cloned.1.call-done = bf16[704,2048]{1,0:T(8,128)(2,1)} async-done(((bf16[704,128]{1,0:T(8,128)(2,1)}), bf16[704,2048]{1,0:T(8,128)(2,1)}) %all-gather.14.cloned.1.call-update) | async-done | bytes 2883600 | tf_op jit(solution)/shard_map/all_gather | solution.py:172
  396.9 12.0 %convolution_convert_fusion.1 = bf16[1024,2048]{1,0:T(8,128)(2,1)} fusion(bf16[704,2048]{1,0:T(8,128)(2,1)} %all-gather.14.cloned.1.call-done, f32[1024,704]{0,1:T(8,128)} %fusion.114, bf16[1024,2048]{1,0:T(8,128)(2,1)} %all-gather.8.cloned.1.call-done, bf16[2048,704]{0,1:T(8,128)(2,1)} %all-gather.12.cloned.1.call-done), kind=kOutput, calls=%fused_computation.94 | convolution fusion | flops 5912002560 | bytes 17039360 | tf_op jit(solution)/shard_map/dot_general | solution.py:178
  409.5 21.5 %reduce-scatter.10.cloned.1.call-done = bf16[512,3]{1,0:T(8,128)(2,1)} async-done(((bf16[4096,3]{1,0:T(8,128)(2,1)}), bf16[512,3]{1,0:T(8,128)(2,1)}) %reduce-scatter.10.cloned.1.call-update) | async-done | bytes 3088
  431.0 1.6 copy.251
  432.6 31.0 %reduce-scatter.8.cloned.1.call-done = bf16[1,128,256]{2,1,0:T(8,128)(2,1)} async-done(((bf16[8,128,256]{2,1,0:T(8,128)(2,1)}), bf16[1,128,256]{2,1,0:T(8,128)(2,1)}) %reduce-scatter.8.cloned.1.call-update) | async-done | bytes 65552 | tf_op jit(solution)/shard_map/reduce_scatter | solution.py:144
  463.6 1.5 bitcast_convert_fusion
  465.1 37.8 %reduce-scatter.6.cloned.1.call-done = bf16[128,2048]{1,0:T(8,128)(2,1)} async-done(((bf16[1024,2048]{1,0:T(8,128)(2,1)}), bf16[128,2048]{1,0:T(8,128)(2,1)}) %reduce-scatter.6.cloned.1.call-update) | async-done | bytes 524304 | tf_op jit(solution)/shard_map/reduce_scatter | solution.py:177
  502.9 2.0 fusion.82
  (177 shorter events, 68.4 us)
Async XLA Ops:
  7.2 198.2 %copy-start = (f32[256]{0:T(256)S(1)}, f32[256]{0:T(256)}, u32[]{:S(2)}) copy-start(f32[256]{0:T(256)} %param.38) | copy-start | bytes 3076
  7.2 233.8 %all-gather.6.cloned.1.call-start = ((), (), s32[]{:S(2)}) async-start(), calls=%async_computation.3 | async-start | bytes 8454144 | tf_op jit(solution)/shard_map/all_gather | solution.py:160
  8.1 9.1 %collective-permute-start = (bf16[3,4096]{1,0:T(4,128)(2,1)S(1)}, bf16[3,4096]{1,0:T(4,128)(2,1)S(1)}, u32[]{:S(2)}, u32[]{:S(2)}) collective-permute-start(bf16[3,4096]{1,0:T(4,128)(2,1)S(1)} %slice_bitcast_fusion.2), channel_id=1, source_target_pairs={{0,1},{1,2},{2,3},{3,4},{4,5},{5,6},{6,7},{8,9},{9,10},{10,11},{11... | collective-permute-start | bytes 73736 | tf_op jit(solution)/shard_map/ppermute | solution.py:20
  9.4 249.4 %all-gather.10.cloned.1.call-start = ((), (), s32[]{:S(2)}) async-start(), calls=%async_computation.5 | async-start | bytes 3063808 | tf_op jit(solution)/shard_map/all_gather | solution.py:169
  20.6 1.7 copy-start.2
  23.9 83.9 %copy-start.9 = (f32[8,2,64,128]{3,0,2,1:T(8,128)}, f32[8,2,64,128]{3,0,2,1:T(8,128)S(1)}, u32[]{:S(2)}) copy-start(f32[8,2,64,128]{3,0,2,1:T(8,128)S(1)} %get-tuple-element.663) | copy-start | bytes 1572868
  23.9 85.7 %slice-start = ((f32[128,4096]{1,0:T(8,128)}), f32[128,2048]{1,0:T(8,128)S(1)}, s32[]{:S(2)}) async-start(f32[128,4096]{1,0:T(8,128)} %copy-done.2), calls=%async_computation.11 | async-start | bytes 2097152 | tf_op jit(solution)/shard_map/slice | solution.py:125
  116.8 6.6 %collective-permute-start.1 = (bf16[8,128,256]{2,1,0:T(8,128)(2,1)}, bf16[8,128,256]{2,1,0:T(8,128)(2,1)}, u32[]{:S(2)}, u32[]{:S(2)}) collective-permute-start(bf16[8,128,256]{2,1,0:T(8,128)(2,1)} %convert_element_type.129), channel_id=1, source_target_pairs={{0,1},{1,2},{2,3},{3,4},{4,5},{5,6},{6,7},{8,9},{9,10},{10,11},{11... | collective-permute-start | bytes 1572872 | tf_op jit(solution)/shard_map/ppermute | solution.py:20
  129.6 8.3 %collective-permute-start.2 = (bf16[8,128,256]{2,1,0:T(8,128)(2,1)}, bf16[8,128,256]{2,1,0:T(8,128)(2,1)}, u32[]{:S(2)}, u32[]{:S(2)}) collective-permute-start(bf16[8,128,256]{2,1,0:T(8,128)(2,1)} %convert_element_type.131), channel_id=1, source_target_pairs={{0,1},{1,2},{2,3},{3,4},{4,5},{5,6},{6,7},{8,9},{9,10},{10,11},{11... | collective-permute-start | bytes 1572872 | tf_op jit(solution)/shard_map/ppermute | solution.py:20
  144.2 10.8 %collective-permute-start.3 = (bf16[8,128,256]{2,1,0:T(8,128)(2,1)}, bf16[8,128,256]{2,1,0:T(8,128)(2,1)}, u32[]{:S(2)}, u32[]{:S(2)}) collective-permute-start(bf16[8,128,256]{2,1,0:T(8,128)(2,1)} %convert_element_type.133), channel_id=1, source_target_pairs={{0,1},{1,2},{2,3},{3,4},{4,5},{5,6},{6,7},{8,9},{9,10},{10,11},{11... | collective-permute-start | bytes 1572872 | tf_op jit(solution)/shard_map/ppermute | solution.py:20
  161.2 10.8 %collective-permute-start.4 = (bf16[8,128,256]{2,1,0:T(8,128)(2,1)}, bf16[8,128,256]{2,1,0:T(8,128)(2,1)}, u32[]{:S(2)}, u32[]{:S(2)}) collective-permute-start(bf16[8,128,256]{2,1,0:T(8,128)(2,1)} %convert_element_type.135), channel_id=1, source_target_pairs={{0,1},{1,2},{2,3},{3,4},{4,5},{5,6},{6,7},{8,9},{9,10},{10,11},{11... | collective-permute-start | bytes 1572872 | tf_op jit(solution)/shard_map/ppermute | solution.py:20
  178.3 10.8 %collective-permute-start.5 = (bf16[8,128,256]{2,1,0:T(8,128)(2,1)}, bf16[8,128,256]{2,1,0:T(8,128)(2,1)}, u32[]{:S(2)}, u32[]{:S(2)}) collective-permute-start(bf16[8,128,256]{2,1,0:T(8,128)(2,1)} %convert_element_type.137), channel_id=1, source_target_pairs={{0,1},{1,2},{2,3},{3,4},{4,5},{5,6},{6,7},{8,9},{9,10},{10,11},{11... | collective-permute-start | bytes 1572872 | tf_op jit(solution)/shard_map/ppermute | solution.py:20
  195.2 13.6 %collective-permute-start.6 = (bf16[8,128,256]{2,1,0:T(8,128)(2,1)}, bf16[8,128,256]{2,1,0:T(8,128)(2,1)}, u32[]{:S(2)}, u32[]{:S(2)}) collective-permute-start(bf16[8,128,256]{2,1,0:T(8,128)(2,1)} %convert_element_type.139), channel_id=1, source_target_pairs={{0,1},{1,2},{2,3},{3,4},{4,5},{5,6},{6,7},{8,9},{9,10},{10,11},{11... | collective-permute-start | bytes 1572872 | tf_op jit(solution)/shard_map/ppermute | solution.py:20
  205.0 87.8 %all-gather.8.cloned.1.call-start = ((), (), s32[]{:S(2)}) async-start(), calls=%async_computation.4 | async-start | bytes 4718592 | tf_op jit(solution)/shard_map/all_gather | solution.py:173
  214.2 7.6 %copy-start.4 = (f32[16,8,8,128]{3,2,1,0:T(8,128)S(1)}, f32[16,8,8,128]{3,2,1,0:T(8,128)}, u32[]{:S(2)}) copy-start(f32[16,8,8,128]{3,2,1,0:T(8,128)} %copy.258) | copy-start | bytes 1572868
  214.2 8.8 %copy-start.10 = (f32[8,2,64,128]{3,0,2,1:T(8,128)S(1)}, f32[8,2,64,128]{3,0,2,1:T(8,128)}, u32[]{:S(2)}) copy-start(f32[8,2,64,128]{3,0,2,1:T(8,128)} %copy-done.9) | copy-start | bytes 1572868
  214.2 10.6 %collective-permute-start.7 = (bf16[8,128,256]{2,1,0:T(8,128)(2,1)S(1)}, bf16[8,128,256]{2,1,0:T(8,128)(2,1)S(1)}, u32[]{:S(2)}, u32[]{:S(2)}) collective-permute-start(bf16[8,128,256]{2,1,0:T(8,128)(2,1)S(1)} %convert_element_type.141), channel_id=1, source_target_pairs={{0,1},{1,2},{2,3},{3,4},{4,5},{5,6},{6,7},{8,9},{9,10},{10,11},{11... | collective-permute-start | bytes 1572872 | tf_op jit(solution)/shard_map/ppermute | solution.py:20
  224.9 2.3 copy-start.3
  225.0 2.3 copy-start.6
  228.0 1.0 copy-start.7
  230.4 2.3 copy-start.3
  230.4 2.3 copy-start.6
  233.4 1.0 copy-start.7
  235.8 3.3 copy-start.8
  241.0 5.8 %copy-start.11 = (f32[2048]{0:T(1024)S(1)}, f32[2048]{0:T(1024)}, u32[]{:S(2)}) copy-start(f32[2048]{0:T(1024)} %param.40) | copy-start | bytes 24580
  241.0 8.6 %copy-start.5 = (bf16[1,128,4096]{2,1,0:T(8,128)(2,1)S(1)}, bf16[1,128,4096]{2,1,0:T(8,128)(2,1)}, u32[]{:S(2)}) copy-start(bf16[1,128,4096]{2,1,0:T(8,128)(2,1)} %param.30) | copy-start | bytes 3145732
  247.8 97.3 %all-gather.12.cloned.1.call-start = ((), (), s32[]{:S(2)}) async-start(), calls=%async_computation.6 | async-start | bytes 3063808 | tf_op jit(solution)/shard_map/all_gather | solution.py:170
  248.4 148.5 %all-gather.14.cloned.1.call-start = ((), (), s32[]{:S(2)}) async-start(), calls=%async_computation.7 | async-start | bytes 3063808 | tf_op jit(solution)/shard_map/all_gather | solution.py:172
  249.0 182.0 %reduce-scatter.10.cloned.1.call-start = ((), (), s32[]{:S(2)}) async-start(), calls=%async_computation.10 | async-start | bytes 1179648
  251.3 212.2 %reduce-scatter.8.cloned.1.call-start = ((), (), s32[]{:S(2)}) async-start(), calls=%async_computation.9 | async-start | bytes 589824 | tf_op jit(solution)/shard_map/reduce_scatter | solution.py:144
  252.3 250.5 %reduce-scatter.6.cloned.1.call-start = ((), (), s32[]{:S(2)}) async-start(), calls=%async_computation.8 | async-start | bytes 4718592 | tf_op jit(solution)/shard_map/reduce_scatter | solution.py:177
  408.9 96.0 %copy-start.1 = (f32[256]{0:T(256)S(1)}, f32[256]{0:T(256)}, u32[]{:S(2)}) copy-start(f32[256]{0:T(256)} %param.38) | copy-start | bytes 3076
Sparse Core Ops, SparseCore 0:
  11.0 74.0 all-gather.5
  205.1 53.6 all-gather.9
  261.1 31.6 all-gather.7
  294.8 50.2 all-gather.11
  347.0 49.8 all-gather.13
  399.2 31.8 reduce-scatter.9
  433.4 30.1 reduce-scatter.7
  466.0 36.8 reduce-scatter.5
where the time goes:
time: 521 us; the launch traced here: 512 us
  waiting for transfers between devices  233 us (45%)
  other arithmetic  114 us (22%)
  matrix products  71.7 us (14%)
  starting transfers between devices  60.5 us (12%)
  local copies, waits for them, and re-layouts  16.5 us (3%)
  between operations  15.4 us (3%)
    another operation x4, other arithmetic, block_tables(): lax.linalg.triangular_solve(identity + couple, identity, left_side=True,...  80.1 us
    ppermute x8, starting transfers between devices, shifted(): lax.ppermute(value, axis, [(source, source + steps) for source in range(i...  59.8 us
    all_gather x1, waiting for transfers between devices, local(): down_full = lax.all_gather(w_down, 'req', axis=1, tiled=True)  51.8 us
    all_gather x1, waiting for transfers between devices, local(): lax.all_gather(w_up, 'req', axis=0, tiled=True)  44.4 us
    reduce_scatter x1, waiting for transfers between devices, local(): lax.psum_scatter(jnp.dot(inner_units, down_full, preferred_element_type=j...  37.8 us
    all_gather x1, waiting for transfers between devices, local(): shard_rows = lax.all_gather(normed, 'seq', axis=0, tiled=True)  34 us
    reduce_scatter x1, waiting for transfers between devices, local(): lax.psum_scatter(state_term.astype(jnp.bfloat16), 'seq', scatter_dimensio...  31 us
    unnamed x9, waiting for transfers between devices  22.7 us
  transfers between devices with their start and end apart: 16, of which 12 were waited for; matrix products, arithmetic and copies ran while one was open for 39% of the time, Pallas kernels for 0%

commit v1 on v0

--- a/solution.py
+++ b/solution.py
@@ -12,6 +12,11 @@
 EPS_NORM = 1e-05
 EPS_UNIT = 1e-06
 HIGHEST = lax.Precision.HIGHEST
+
+
+def all_by_exchange(block, axis, along):
+    sent = jnp.stack([block] * lax.axis_size(axis))
+    return jnp.concatenate(lax.all_to_all(sent, axis, 0, 0), axis=along)
 
 
 def shifted(value, axis, steps):
@@ -169,7 +174,7 @@
         lax.all_gather(w_gate, "req", axis=0, tiled=True),
         lax.all_gather(w_up, "req", axis=0, tiled=True),
     )
-    down_full = lax.all_gather(w_down, "req", axis=1, tiled=True)
+    down_full = all_by_exchange(w_down, "req", 1)
     shard_rows = lax.all_gather(normed, "seq", axis=0, tiled=True)
     gate_part = jnp.dot(shard_rows, gate_full, preferred_element_type=jnp.float32)
     upward = jnp.dot(shard_rows, up_full, preferred_element_type=jnp.float32)

time: 521 us -> 478 us (0.917)
  waiting for transfers between devices: 233 us -> 179 us
  starting transfers between devices: 60.5 us -> 67.6 us
    all_gather x1 -> x0, waiting for transfers between devices: 51.8 us -> none  [local(): down_full = lax.all_gather(w_down, 'req', axis=1, tiled=True)]
    all_to_all x0 -> x1, starting transfers between devices: none -> 7.19 us  [all_by_exchange(): return jnp.concatenate(lax.all_to_all(sent, axis, 0, 0), axis=along)]
    all_gather x1, waiting for transfers between devices: 6.25 us -> 0.02 us  [local(): lax.all_gather(w_gate, 'req', axis=0, tiled=True)]
    unnamed x32 -> x40, local copies, waits for them, and re-layouts: 9.73 us -> 10.5 us
    unnamed x9 -> x8, waiting for transfers between devices: 22.7 us -> 22 us
  transfers between devices with their start and end apart: 16 -> 16, of which waited for: 12 -> 10; matrix products, arithmetic and copies ran while one was open for 39% -> 43% of each run, Pallas kernels for 0% -> 0%
where the time goes in v1:
time: 478 us; the launch traced here: 470 us
  waiting for transfers between devices  179 us (37%)
  other arithmetic  116 us (24%)
  matrix products  71.6 us (15%)
  starting transfers between devices  67.6 us (14%)
  local copies, waits for them, and re-layouts  19.4 us (4%)
  between operations  15.6 us (3%)
    another operation x4, other arithmetic, block_tables(): lax.linalg.triangular_solve(identity + couple, identity, left_side=True,...  80.7 us
    ppermute x8, starting transfers between devices, shifted(): lax.ppermute(value, axis, [(source, source + steps) for source in range(i...  59.7 us
    all_gather x1, waiting for transfers between devices, local(): lax.all_gather(w_up, 'req', axis=0, tiled=True)  44.4 us
    all_gather x1, waiting for transfers between devices, local(): shard_rows = lax.all_gather(normed, 'seq', axis=0, tiled=True)  38.7 us
    reduce_scatter x1, waiting for transfers between devices, local(): lax.psum_scatter(jnp.dot(inner_units, down_full, preferred_element_type=j...  37.8 us
    reduce_scatter x1, waiting for transfers between devices, local(): lax.psum_scatter(state_term.astype(jnp.bfloat16), 'seq', scatter_dimensio...  30.8 us
    unnamed x8, waiting for transfers between devices  22 us
    dot_general x16, matrix products, advance(): jnp.einsum('hck,hcx->hkx', keys_now, corrected, precision=HIGHEST)  21.1 us
  transfers between devices with their start and end apart: 16, of which 10 were waited for; matrix products, arithmetic and copies ran while one was open for 43% of the time, Pallas kernels for 0%

profile of v1, /device:TPU:0, one launch (start us, length us, event | category | flops | bytes accessed | tf_op | source)
XLA Modules:
  0.0 469.5 jit_solution(6112004581645283876)
XLA Ops:
  12.3 2.0 fusion.108
  17.9 3.4 divide_multiply_fusion
  21.3 1.4 multiply_bitcast_fusion
  27.4 1.8 fusion.74
  29.2 80.0 %custom-call.3 = f32[8,2,1,64,64]{3,4,2,1,0:T(8,128)} custom-call(f32[8,2,1,64,64]{4,3,2,1,0:T(8,128)} %fusion.74), custom_call_target="InvertDiagBlocksLowerTriangular" | custom-call | tf_op jit(solution)/shard_map/triangular_solve | solution.py:50
  109.2 2.0 fusion.87
  111.2 1.7 convolution_bitcast_fusion.2
  115.3 4.1 while.90
  120.3 5.9 %collective-permute-start.1 = (bf16[8,128,256]{2,1,0:T(8,128)(2,1)}, bf16[8,128,256]{2,1,0:T(8,128)(2,1)}, u32[]{:S(2)}, u32[]{:S(2)}) collective-permute-start(bf16[8,128,256]{2,1,0:T(8,128)(2,1)} %convert_element_type.129), channel_id=1, source_target_pairs={{0,1},{1,2},{2,3},{3,4},{4,5},{5,6},{6,7},{8,9},{9,10},{10,11},{11... | collective-permute-start | bytes 1572872 | tf_op jit(solution)/shard_map/ppermute | solution.py:25
  128.0 4.2 while.83
  130.8 1.3 convolution_add_fusion.18
  133.1 7.3 %collective-permute-start.2 = (bf16[8,128,256]{2,1,0:T(8,128)(2,1)}, bf16[8,128,256]{2,1,0:T(8,128)(2,1)}, u32[]{:S(2)}, u32[]{:S(2)}) collective-permute-start(bf16[8,128,256]{2,1,0:T(8,128)(2,1)} %convert_element_type.131), channel_id=1, source_target_pairs={{0,1},{1,2},{2,3},{3,4},{4,5},{5,6},{6,7},{8,9},{9,10},{10,11},{11... | collective-permute-start | bytes 1572872 | tf_op jit(solution)/shard_map/ppermute | solution.py:25
  142.6 4.2 while.84
  143.3 1.3 convolution_add_fusion.19
  147.7 9.7 %collective-permute-start.3 = (bf16[8,128,256]{2,1,0:T(8,128)(2,1)}, bf16[8,128,256]{2,1,0:T(8,128)(2,1)}, u32[]{:S(2)}, u32[]{:S(2)}) collective-permute-start(bf16[8,128,256]{2,1,0:T(8,128)(2,1)} %convert_element_type.133), channel_id=1, source_target_pairs={{0,1},{1,2},{2,3},{3,4},{4,5},{5,6},{6,7},{8,9},{9,10},{10,11},{11... | collective-permute-start | bytes 1572872 | tf_op jit(solution)/shard_map/ppermute | solution.py:25
  159.6 4.2 while.85
  160.4 1.3 convolution_add_fusion.20
  164.7 9.7 %collective-permute-start.4 = (bf16[8,128,256]{2,1,0:T(8,128)(2,1)}, bf16[8,128,256]{2,1,0:T(8,128)(2,1)}, u32[]{:S(2)}, u32[]{:S(2)}) collective-permute-start(bf16[8,128,256]{2,1,0:T(8,128)(2,1)} %convert_element_type.135), channel_id=1, source_target_pairs={{0,1},{1,2},{2,3},{3,4},{4,5},{5,6},{6,7},{8,9},{9,10},{10,11},{11... | collective-permute-start | bytes 1572872 | tf_op jit(solution)/shard_map/ppermute | solution.py:25
  176.7 4.2 while.86
  177.4 1.3 convolution_add_fusion.21
  181.8 9.7 %collective-permute-start.5 = (bf16[8,128,256]{2,1,0:T(8,128)(2,1)}, bf16[8,128,256]{2,1,0:T(8,128)(2,1)}, u32[]{:S(2)}, u32[]{:S(2)}) collective-permute-start(bf16[8,128,256]{2,1,0:T(8,128)(2,1)} %convert_element_type.137), channel_id=1, source_target_pairs={{0,1},{1,2},{2,3},{3,4},{4,5},{5,6},{6,7},{8,9},{9,10},{10,11},{11... | collective-permute-start | bytes 1572872 | tf_op jit(solution)/shard_map/ppermute | solution.py:25
  193.7 4.2 while.87
  198.8 9.7 %collective-permute-start.6 = (bf16[8,128,256]{2,1,0:T(8,128)(2,1)}, bf16[8,128,256]{2,1,0:T(8,128)(2,1)}, u32[]{:S(2)}, u32[]{:S(2)}) collective-permute-start(bf16[8,128,256]{2,1,0:T(8,128)(2,1)} %convert_element_type.139), channel_id=1, source_target_pairs={{0,1},{1,2},{2,3},{3,4},{4,5},{5,6},{6,7},{8,9},{9,10},{10,11},{11... | collective-permute-start | bytes 1572872 | tf_op jit(solution)/shard_map/ppermute | solution.py:25
  210.5 1.9 copy.262
  213.5 4.2 while.88
  214.3 1.3 convolution_add_fusion.23
  216.4 1.3 convolution_add_fusion.23
  217.8 6.3 %collective-permute-start.7 = (bf16[8,128,256]{2,1,0:T(8,128)(2,1)S(1)}, bf16[8,128,256]{2,1,0:T(8,128)(2,1)S(1)}, u32[]{:S(2)}, u32[]{:S(2)}) collective-permute-start(bf16[8,128,256]{2,1,0:T(8,128)(2,1)S(1)} %convert_element_type.141), channel_id=1, source_target_pairs={{0,1},{1,2},{2,3},{3,4},{4,5},{5,6},{6,7},{8,9},{9,10},{10,11},{11... | collective-permute-start | bytes 1572872 | tf_op jit(solution)/shard_map/ppermute | solution.py:25
  226.5 1.9 fusion.72
  228.5 10.9 %while.89 = (s32[]{:T(128)}, f32[8,128,256]{2,1,0:T(8,128)S(1)}, f32[2,8,64,256]{3,2,1,0:T(8,128)}, f32[2,8]{1,0:T(2,128)S(1)}, f32[2,8,64,128]{3,2,1,0:T(8,128)...) while((s32[]{:T(128)}, f32[8,128,256]{2,1,0:T(8,128)S(1)}, ...), condition=%wide.region_20.21_spmd, body=%wide.region_19.20_spmd.sunk | while | flops 705429504 | bytes 19925256 | solution.py:90
  229.3 1.5 fusion.225
  234.7 1.5 fusion.225
  239.4 1.5 multiply_reduce_fusion.1
  241.2 1.4 copy.265
  243.6 5.5 %multiply_reduce_fusion = (f32[128]{0:T(128)S(1)}, f32[128,2048]{1,0:T(8,128)S(1)}) fusion(bf16[2048,2048]{1,0:T(8,128)(2,1)} %all-gather.5.cloned.1.call-done, f32[128,2048]{1,0:T(8,128)S(1)} %bitcast.355, f32[128,2048]{1,0:T(8,128)} %bitcast.354, bf16[1,128,2048]{2,1,0:T(8,128)(2,1)} %param.31, f32[2048]{0:T(1024)S(1)} %bitcast.367, ...), kind=kOutput, calls=%fused_computation.127 | convolution fusion | flops 1077673856 | bytes 12591616 | tf_op jit(solution)/shard_map/dot_general | solution.py:163
  250.7 2.2 stack.2
  252.9 7.2 %all-to-all-start = ((bf16[16,704,128]{2,1,0:T(8,128)(2,1)}), bf16[16,704,128]{2,1,0:T(8,128)(2,1)}, u32[]{:S(2)}, u32[]{:S(2)}) async-start(bf16[16,704,128]{2,1,0:T(8,128)(2,1)} %stack.2), calls=%async_computation | async-start | bytes 5767168 | tf_op jit(solution)/shard_map/all_to_all | solution.py:19
  261.3 1.4 copy.253
  263.8 38.7 %all-gather.7.cloned.1.call-done = bf16[1024,2048]{1,0:T(8,128)(2,1)} async-done(((bf16[128,2048]{1,0:T(8,128)(2,1)}), bf16[1024,2048]{1,0:T(8,128)(2,1)}) %all-gather.7.cloned.1.call-update) | async-done | bytes 4194320 | tf_op jit(solution)/shard_map/all_gather | solution.py:178
  302.4 7.8 %fusion.116 = f32[1024,704]{0,1:T(8,128)} fusion(bf16[1024,2048]{1,0:T(8,128)(2,1)} %all-gather.7.cloned.1.call-done, bf16[2048,704]{0,1:T(8,128)(2,1)} %all-gather.9.cloned.1.call-done), kind=kOutput, calls=%fused_computation.197 | convolution fusion | flops 2952790016 | bytes 9961472 | tf_op jit(solution)/shard_map/dot_general | solution.py:179
  310.3 44.4 %all-gather.11.cloned.1.call-done = bf16[2048,704]{0,1:T(8,128)(2,1)} async-done(((bf16[128,704]{0,1:T(8,128)(2,1)}), bf16[2048,704]{0,1:T(8,128)(2,1)}) %all-gather.11.cloned.1.call-update) | async-done | bytes 2883600 | tf_op jit(solution)/shard_map/all_gather | solution.py:175
  354.7 12.0 %convolution_convert_fusion.1 = bf16[1024,2048]{1,0:T(8,128)(2,1)} fusion(f32[1024,704]{0,1:T(8,128)} %fusion.116, bf16[1024,2048]{1,0:T(8,128)(2,1)} %all-gather.7.cloned.1.call-done, bf16[2048,704]{0,1:T(8,128)(2,1)} %all-gather.11.cloned.1.call-done, bf16[16,704,128]{2,1,0:T(8,128)(2,1)} %all-to-all-done), kind=kOutput, calls=%fused_computation.94 | convolution fusion | flops 5912002560 | bytes 17039360 | tf_op jit(solution)/shard_map/dot_general | solution.py:183
  367.4 21.4 %reduce-scatter.10.cloned.1.call-done = bf16[512,3]{1,0:T(8,128)(2,1)} async-done(((bf16[4096,3]{1,0:T(8,128)(2,1)}), bf16[512,3]{1,0:T(8,128)(2,1)}) %reduce-scatter.10.cloned.1.call-update) | async-done | bytes 3088
  388.8 1.6 copy.254
  390.4 30.8 %reduce-scatter.8.cloned.1.call-done = bf16[1,128,256]{2,1,0:T(8,128)(2,1)} async-done(((bf16[8,128,256]{2,1,0:T(8,128)(2,1)}), bf16[1,128,256]{2,1,0:T(8,128)(2,1)}) %reduce-scatter.8.cloned.1.call-update) | async-done | bytes 65552 | tf_op jit(solution)/shard_map/reduce_scatter | solution.py:149
  421.2 1.5 bitcast_convert_fusion
  422.7 37.8 %reduce-scatter.6.cloned.1.call-done = bf16[128,2048]{1,0:T(8,128)(2,1)} async-done(((bf16[1024,2048]{1,0:T(8,128)(2,1)}), bf16[128,2048]{1,0:T(8,128)(2,1)}) %reduce-scatter.6.cloned.1.call-update) | async-done | bytes 524304 | tf_op jit(solution)/shard_map/reduce_scatter | solution.py:182
  460.5 2.0 fusion.84
  (185 shorter events, 70.5 us)
Async XLA Ops:
  7.2 201.7 %copy-start = (f32[256]{0:T(256)S(1)}, f32[256]{0:T(256)}, u32[]{:S(2)}) copy-start(f32[256]{0:T(256)} %param.38) | copy-start | bytes 3076
  7.2 236.4 %all-gather.5.cloned.1.call-start = ((), (), s32[]{:S(2)}) async-start(), calls=%async_computation.4 | async-start | bytes 8454144 | tf_op jit(solution)/shard_map/all_gather | solution.py:165
  8.1 9.8 %collective-permute-start = (bf16[3,4096]{1,0:T(4,128)(2,1)S(1)}, bf16[3,4096]{1,0:T(4,128)(2,1)S(1)}, u32[]{:S(2)}, u32[]{:S(2)}) collective-permute-start(bf16[3,4096]{1,0:T(4,128)(2,1)S(1)} %slice_bitcast_fusion.2), channel_id=1, source_target_pairs={{0,1},{1,2},{2,3},{3,4},{4,5},{5,6},{6,7},{8,9},{9,10},{10,11},{11... | collective-permute-start | bytes 73736 | tf_op jit(solution)/shard_map/ppermute | solution.py:25
  9.4 254.4 %all-gather.9.cloned.1.call-start = ((), (), s32[]{:S(2)}) async-start(), calls=%async_computation.6 | async-start | bytes 3063808 | tf_op jit(solution)/shard_map/all_gather | solution.py:174
  21.3 2.3 copy-start.2
  22.7 4.6 copy-start.15
  26.2 85.0 %copy-start.5 = (f32[16,8,8,128]{3,2,1,0:T(8,128)}, f32[16,8,8,128]{3,2,1,0:T(8,128)S(1)}, u32[]{:S(2)}) copy-start(f32[16,8,8,128]{3,2,1,0:T(8,128)S(1)} %copy.259) | copy-start | bytes 1572868
  27.4 1.8 copy-start.11
  27.4 85.7 %slice-start = ((f32[128,4096]{1,0:T(8,128)}), f32[128,2048]{1,0:T(8,128)S(1)}, s32[]{:S(2)}) async-start(f32[128,4096]{1,0:T(8,128)} %copy-done.2), calls=%async_computation.11 | async-start | bytes 2097152 | tf_op jit(solution)/shard_map/slice | solution.py:130
  113.4 1.4 copy-start.6
  120.3 6.5 %collective-permute-start.1 = (bf16[8,128,256]{2,1,0:T(8,128)(2,1)}, bf16[8,128,256]{2,1,0:T(8,128)(2,1)}, u32[]{:S(2)}, u32[]{:S(2)}) collective-permute-start(bf16[8,128,256]{2,1,0:T(8,128)(2,1)} %convert_element_type.129), channel_id=1, source_target_pairs={{0,1},{1,2},{2,3},{3,4},{4,5},{5,6},{6,7},{8,9},{9,10},{10,11},{11... | collective-permute-start | bytes 1572872 | tf_op jit(solution)/shard_map/ppermute | solution.py:25
  133.1 8.3 %collective-permute-start.2 = (bf16[8,128,256]{2,1,0:T(8,128)(2,1)}, bf16[8,128,256]{2,1,0:T(8,128)(2,1)}, u32[]{:S(2)}, u32[]{:S(2)}) collective-permute-start(bf16[8,128,256]{2,1,0:T(8,128)(2,1)} %convert_element_type.131), channel_id=1, source_target_pairs={{0,1},{1,2},{2,3},{3,4},{4,5},{5,6},{6,7},{8,9},{9,10},{10,11},{11... | collective-permute-start | bytes 1572872 | tf_op jit(solution)/shard_map/ppermute | solution.py:25
  147.7 10.8 %collective-permute-start.3 = (bf16[8,128,256]{2,1,0:T(8,128)(2,1)}, bf16[8,128,256]{2,1,0:T(8,128)(2,1)}, u32[]{:S(2)}, u32[]{:S(2)}) collective-permute-start(bf16[8,128,256]{2,1,0:T(8,128)(2,1)} %convert_element_type.133), channel_id=1, source_target_pairs={{0,1},{1,2},{2,3},{3,4},{4,5},{5,6},{6,7},{8,9},{9,10},{10,11},{11... | collective-permute-start | bytes 1572872 | tf_op jit(solution)/shard_map/ppermute | solution.py:25
  164.7 10.8 %collective-permute-start.4 = (bf16[8,128,256]{2,1,0:T(8,128)(2,1)}, bf16[8,128,256]{2,1,0:T(8,128)(2,1)}, u32[]{:S(2)}, u32[]{:S(2)}) collective-permute-start(bf16[8,128,256]{2,1,0:T(8,128)(2,1)} %convert_element_type.135), channel_id=1, source_target_pairs={{0,1},{1,2},{2,3},{3,4},{4,5},{5,6},{6,7},{8,9},{9,10},{10,11},{11... | collective-permute-start | bytes 1572872 | tf_op jit(solution)/shard_map/ppermute | solution.py:25
  181.8 10.8 %collective-permute-start.5 = (bf16[8,128,256]{2,1,0:T(8,128)(2,1)}, bf16[8,128,256]{2,1,0:T(8,128)(2,1)}, u32[]{:S(2)}, u32[]{:S(2)}) collective-permute-start(bf16[8,128,256]{2,1,0:T(8,128)(2,1)} %convert_element_type.137), channel_id=1, source_target_pairs={{0,1},{1,2},{2,3},{3,4},{4,5},{5,6},{6,7},{8,9},{9,10},{10,11},{11... | collective-permute-start | bytes 1572872 | tf_op jit(solution)/shard_map/ppermute | solution.py:25
  198.8 13.6 %collective-permute-start.6 = (bf16[8,128,256]{2,1,0:T(8,128)(2,1)}, bf16[8,128,256]{2,1,0:T(8,128)(2,1)}, u32[]{:S(2)}, u32[]{:S(2)}) collective-permute-start(bf16[8,128,256]{2,1,0:T(8,128)(2,1)} %convert_element_type.139), channel_id=1, source_target_pairs={{0,1},{1,2},{2,3},{3,4},{4,5},{5,6},{6,7},{8,9},{9,10},{10,11},{11... | collective-permute-start | bytes 1572872 | tf_op jit(solution)/shard_map/ppermute | solution.py:25
  208.5 93.9 %all-gather.7.cloned.1.call-start = ((), (), s32[]{:S(2)}) async-start(), calls=%async_computation.5 | async-start | bytes 4718592 | tf_op jit(solution)/shard_map/all_gather | solution.py:178
  217.7 7.7 %copy-start.4 = (f32[16,8,8,128]{3,2,1,0:T(8,128)S(1)}, f32[16,8,8,128]{3,2,1,0:T(8,128)}, u32[]{:S(2)}) copy-start(f32[16,8,8,128]{3,2,1,0:T(8,128)} %copy.262) | copy-start | bytes 1572868
  217.7 8.8 %copy-start.12 = (f32[8,2,64,128]{3,0,2,1:T(8,128)S(1)}, f32[8,2,64,128]{3,0,2,1:T(8,128)}, u32[]{:S(2)}) copy-start(f32[8,2,64,128]{3,0,2,1:T(8,128)} %copy-done.11) | copy-start | bytes 1572868
  217.8 10.6 %collective-permute-start.7 = (bf16[8,128,256]{2,1,0:T(8,128)(2,1)S(1)}, bf16[8,128,256]{2,1,0:T(8,128)(2,1)S(1)}, u32[]{:S(2)}, u32[]{:S(2)}) collective-permute-start(bf16[8,128,256]{2,1,0:T(8,128)(2,1)S(1)} %convert_element_type.141), channel_id=1, source_target_pairs={{0,1},{1,2},{2,3},{3,4},{4,5},{5,6},{6,7},{8,9},{9,10},{10,11},{11... | collective-permute-start | bytes 1572872 | tf_op jit(solution)/shard_map/ppermute | solution.py:25
  228.5 2.3 copy-start.3
  228.5 2.3 copy-start.8
  231.6 1.0 copy-start.9
  233.9 2.3 copy-start.3
  233.9 2.3 copy-start.8
  237.0 1.0 copy-start.9
  239.4 3.2 copy-start.10
  243.6 5.5 %copy-start.14 = (f32[2048]{0:T(1024)S(1)}, f32[2048]{0:T(1024)}, u32[]{:S(2)}) copy-start(f32[2048]{0:T(1024)} %param.40) | copy-start | bytes 24580
  243.6 7.1 %copy-start.13 = (bf16[704,128]{1,0:T(8,128)(2,1)S(1)}, bf16[704,128]{1,0:T(8,128)(2,1)}, u32[]{:S(2)}) copy-start(bf16[704,128]{1,0:T(8,128)(2,1)} %param.43) | copy-start | bytes 540676
  250.1 104.6 %all-gather.11.cloned.1.call-start = ((), (), s32[]{:S(2)}) async-start(), calls=%async_computation.7 | async-start | bytes 3063808 | tf_op jit(solution)/shard_map/all_gather | solution.py:175
  252.9 8.1 %copy-start.7 = (bf16[1,128,4096]{2,1,0:T(8,128)(2,1)S(1)}, bf16[1,128,4096]{2,1,0:T(8,128)(2,1)}, u32[]{:S(2)}) copy-start(bf16[1,128,4096]{2,1,0:T(8,128)(2,1)} %param.30) | copy-start | bytes 3145732
  252.9 57.4 %all-to-all-start = ((bf16[16,704,128]{2,1,0:T(8,128)(2,1)}), bf16[16,704,128]{2,1,0:T(8,128)(2,1)}, u32[]{:S(2)}, u32[]{:S(2)}) async-start(bf16[16,704,128]{2,1,0:T(8,128)(2,1)} %stack.2), calls=%async_computation | async-start | bytes 5767168 | tf_op jit(solution)/shard_map/all_to_all | solution.py:19
  260.1 128.7 %reduce-scatter.10.cloned.1.call-start = ((), (), s32[]{:S(2)}) async-start(), calls=%async_computation.10 | async-start | bytes 1179648
  262.7 158.5 %reduce-scatter.8.cloned.1.call-start = ((), (), s32[]{:S(2)}) async-start(), calls=%async_computation.9 | async-start | bytes 589824 | tf_op jit(solution)/shard_map/reduce_scatter | solution.py:149
  263.7 196.8 %reduce-scatter.6.cloned.1.call-start = ((), (), s32[]{:S(2)}) async-start(), calls=%async_computation.8 | async-start | bytes 4718592 | tf_op jit(solution)/shard_map/reduce_scatter | solution.py:182
  366.7 95.8 %copy-start.1 = (f32[256]{0:T(256)S(1)}, f32[256]{0:T(256)}, u32[]{:S(2)}) copy-start(f32[256]{0:T(256)} %param.38) | copy-start | bytes 3076
Sparse Core Ops, SparseCore 0:
  11.0 73.5 all-gather.4
  208.7 53.6 all-gather.8
  264.7 37.7 all-gather.6
  304.4 50.2 all-gather.10
  356.9 31.7 reduce-scatter.9
  391.0 30.1 reduce-scatter.7
  423.6 36.8 reduce-scatter.5
